TPU v7x, 32 devices: a whole 2x2x4 slice. The times are simulated.
32 devices in a mesh: seq: 8 (over z, y), tensor: 4 (over x, core).
Axes of the slice: x: 2, y: 2, z: 4, core: 2. Of those that a mesh axis runs over, the one named last changes fastest.
Arguments:
- inputs: bfloat16 [1024, 3, 4096], P('seq', None, 'tensor'), may hold values from -6 to 6
- short_taps: float32 [7, 3, 4096], P(None, None, 'tensor'), may hold values from -2 to 2
- medium_taps: float32 [120, 4096], P(None, 'tensor'), may hold values from -0.5 to 0.5
- long_filter: float32 [1024, 4096], P('seq', 'tensor'), may hold values from -4 to 4
- out_weight: bfloat16 [8192, 4096], P(None, 'tensor'), may hold values from -0.09375 to 0.09375
- out_cotangent: bfloat16 [1024, 8192], P('seq', 'tensor'), may hold values from -6 to 6
Outputs:
- output: bfloat16 [1024, 8192], P('seq', 'tensor')
- input_grad: bfloat16 [1024, 3, 4096], P('seq', None, 'tensor')
- filter_grad: float32 [1024, 4096], P('seq', 'tensor')
- medium_grad: float32 [120, 4096], P(None, 'tensor')
- short_grad: float32 [7, 3, 4096], P(None, None, 'tensor')
All inputs are finite; a program needn't handle non-finite values.
Results may differ from a plain program's by a relative error of at most 0.013.
Values may be sent and summed in bfloat16 or wider, within the bound.
No kernel may reach another device: no remote copies, remote signals or barrier semaphores. Data moves between devices by JAX's collectives and lax.ppermute only.
A program may use at most 128 MiB of HBM per device.

v0:
```python
import math
import jax
import jax.numpy as jnp
from jax import lax
from jax.sharding import PartitionSpec as P

precise = lax.Precision.HIGHEST


def from_behind(value, axis, steps):
    count = lax.axis_size(axis)
    leading, last = (max(0, -steps), min(count, count - steps))
    return lax.ppermute(value, axis, [(source, source + steps) for source in range(leading, last)])


def as_sent(shard):

    def short(part):
        return part.astype(jnp.bfloat16) if part.dtype == jnp.float32 else part

    return jax.tree.map(short, shard)


def correlate(signal, kernel):
    channels = kernel.shape[1]
    result = lax.conv_general_dilated(
        signal[None],
        kernel[:, None, :],
        (1,),
        "VALID",
        dimension_numbers=("NWC", "WIO", "NWC"),
        feature_group_count=channels,
        precision=precise,
    )
    return result[0]


def angles(left_index, right_index, modulus):
    return (left_index * right_index % modulus).astype(jnp.float32) * (2.0 * math.pi / modulus)


def to_spectrum(signals, cos_table, sin_table):
    signal_count = signals.shape[0]
    length = signals.shape[1]
    channels = signals.shape[2]
    devices = lax.axis_size("seq")
    position = lax.axis_index("seq")
    stride = length // devices
    modulus = 2 * devices * length
    columns = lax.all_to_all(
        signals.reshape(signal_count, devices, stride, channels),
        "seq",
        split_axis=1,
        concat_axis=1,
        tiled=True,
    )
    coarse = jnp.arange(2 * devices, dtype=jnp.int32)
    sources = jnp.arange(devices, dtype=jnp.int32)
    coarse_angle = angles(coarse[:, None], sources[None, :], 2 * devices)
    first_real = jnp.einsum("kp,spmc->skmc", jnp.cos(coarse_angle), columns, precision=precise)
    first_imag = -jnp.einsum("kp,spmc->skmc", jnp.sin(coarse_angle), columns, precision=precise)
    local_rows = position * stride + jnp.arange(stride, dtype=jnp.int32)
    twiddle = angles(coarse[:, None], local_rows[None, :], modulus)
    cosine_values = jnp.cos(twiddle)[None, :, :, None]
    sine_part = jnp.sin(twiddle)[None, :, :, None]
    turned = jnp.stack(
        [
            first_real * cosine_values + first_imag * sine_part,
            first_imag * cosine_values - first_real * sine_part,
        ]
    )
    arrived = lax.all_to_all(turned, "seq", split_axis=2, concat_axis=3, tiled=True)
    spec_real = jnp.einsum("km,sjmc->sjkc", cos_table, arrived[0], precision=precise) + jnp.einsum(
        "km,sjmc->sjkc", sin_table, arrived[1], precision=precise
    )
    spec_imag = jnp.einsum("km,sjmc->sjkc", cos_table, arrived[1], precision=precise) - jnp.einsum(
        "km,sjmc->sjkc", sin_table, arrived[0], precision=precise
    )
    return (spec_real, spec_imag)


def from_spectrum(spec_real, spec_imag, cos_table, sin_table):
    signal_count = spec_real.shape[0]
    length = spec_real.shape[2]
    channels = spec_real.shape[3]
    devices = lax.axis_size("seq")
    position = lax.axis_index("seq")
    modulus = 2 * devices * length
    fine_real = jnp.einsum("mk,sjkc->sjmc", cos_table, spec_real, precision=precise) - jnp.einsum(
        "mk,sjkc->sjmc", sin_table, spec_imag, precision=precise
    )
    fine_imag = jnp.einsum("mk,sjkc->sjmc", cos_table, spec_imag, precision=precise) + jnp.einsum(
        "mk,sjkc->sjmc", sin_table, spec_real, precision=precise
    )
    held = 2 * position + jnp.arange(2, dtype=jnp.int32)
    all_rows = jnp.arange(length, dtype=jnp.int32)
    twiddle = angles(held[:, None], all_rows[None, :], modulus)
    cosine_values = jnp.cos(twiddle)[None, :, :, None]
    sine_part = jnp.sin(twiddle)[None, :, :, None]
    turned = jnp.stack(
        [
            fine_real * cosine_values - fine_imag * sine_part,
            fine_real * sine_part + fine_imag * cosine_values,
        ]
    )
    arrived = lax.all_to_all(turned, "seq", split_axis=3, concat_axis=2, tiled=True)
    coarse = jnp.arange(2 * devices, dtype=jnp.int32)
    sources = jnp.arange(devices, dtype=jnp.int32)
    coarse_angle = angles(sources[:, None], coarse[None, :], 2 * devices)
    blocks = (
        jnp.einsum("pk,skmc->spmc", jnp.cos(coarse_angle), arrived[0], precision=precise)
        - jnp.einsum("pk,skmc->spmc", jnp.sin(coarse_angle), arrived[1], precision=precise)
    ) / modulus
    returned = lax.all_to_all(blocks, "seq", split_axis=1, concat_axis=1, tiled=True)
    return returned.reshape(signal_count, length, channels)


def local(inputs, short_taps, medium_taps, long_filter, out_weight, out_cotangent):
    length = inputs.shape[0]
    groups = inputs.shape[1]
    channels = inputs.shape[2]
    short_reach = short_taps.shape[0]
    medium_reach = medium_taps.shape[0]
    devices = lax.axis_size("seq")
    scale = 1.0 / math.sqrt(length * devices)
    flat_inputs = inputs.reshape(length, groups * channels)
    short_flat = short_taps.reshape(short_reach, groups * channels)
    input_edge = from_behind(flat_inputs[length - (short_reach - 1) :], "seq", 1)
    extended_inputs = jnp.concatenate([input_edge, flat_inputs], 0).astype(jnp.float32)
    featured = correlate(extended_inputs, short_flat[::-1])
    gated = featured[:, channels : 2 * channels] * featured[:, 2 * channels :]
    gated_edge = from_behind(as_sent(gated[length - (medium_reach - 1) :]), "seq", 1)
    extended_gated = jnp.concatenate([gated_edge, gated], 0)
    query_branch = featured[:, :channels]
    key_branch = featured[:, channels : 2 * channels]
    value_branch = featured[:, 2 * channels :]
    mixed = correlate(extended_gated, medium_taps[::-1])
    all_rows = jnp.arange(length, dtype=jnp.int32)
    grid_angle = angles(all_rows[:, None], all_rows[None, :], length)
    cos_table = jnp.cos(grid_angle)
    sin_table = jnp.sin(grid_angle)
    spec_real, spec_imag = to_spectrum(jnp.stack([mixed, long_filter]), cos_table, sin_table)
    mixed_real = spec_real[0]
    mixed_imag = spec_imag[0]
    filter_real = spec_real[1]
    filter_imag = spec_imag[1]
    conv_real = mixed_real * filter_real - mixed_imag * filter_imag
    conv_imag = mixed_real * filter_imag + mixed_imag * filter_real
    convolved = from_spectrum(conv_real[None], conv_imag[None], cos_table, sin_table)[0]
    product = (query_branch * convolved).astype(jnp.bfloat16)
    partial_out = lax.dot_general(
        product, out_weight, (((1,), (1,)), ((), ())), preferred_element_type=jnp.float32
    )
    output = lax.psum_scatter(partial_out, "tensor", scatter_dimension=1, tiled=True).astype(
        jnp.bfloat16
    )
    full_cotangent = lax.all_gather(out_cotangent, "tensor", axis=1, tiled=True)
    product_grad = jnp.dot(full_cotangent, out_weight, preferred_element_type=jnp.float32)
    query_grad = product_grad * convolved
    convolved_grad = product_grad * query_branch
    grad_real, grad_imag = to_spectrum(convolved_grad[None], cos_table, sin_table)
    grad_real = grad_real[0]
    grad_imag = grad_imag[0]
    back_real = jnp.stack(
        [
            filter_real * grad_real + filter_imag * grad_imag,
            mixed_real * grad_real + mixed_imag * grad_imag,
        ]
    )
    back_imag = jnp.stack(
        [
            filter_real * grad_imag - filter_imag * grad_real,
            mixed_real * grad_imag - mixed_imag * grad_real,
        ]
    )
    timed = from_spectrum(back_real, back_imag, cos_table, sin_table)
    mixed_grad = timed[0]
    filter_grad = timed[1] * scale
    mixed_edge = from_behind(as_sent(mixed_grad[: medium_reach - 1]), "seq", -1)
    gated_grad = correlate(jnp.concatenate([mixed_grad, mixed_edge], 0), medium_taps)
    medium_part = correlate(extended_gated, mixed_grad)[::-1]
    feature_gradient = jnp.concatenate(
        [query_grad, gated_grad * value_branch, gated_grad * key_branch], 1
    )
    featured_edge = from_behind(as_sent(feature_gradient[: short_reach - 1]), "seq", -1)
    input_grad = (
        correlate(jnp.concatenate([feature_gradient, featured_edge], 0), short_flat)
        .astype(jnp.bfloat16)
        .reshape(length, groups, channels)
    )
    short_part = correlate(extended_inputs, feature_gradient)[::-1]
    medium_sum, short_sum = (
        lax.psum(medium_part.astype(jnp.bfloat16), "seq").astype(jnp.float32),
        lax.psum(short_part.astype(jnp.bfloat16), "seq").astype(jnp.float32),
    )
    medium_grad = medium_sum * scale
    short_grad = (short_sum * scale).reshape(short_reach, groups, channels)
    return (output, input_grad, filter_grad, medium_grad, short_grad)


def solution(mesh):
    return jax.shard_map(
        local,
        mesh=mesh,
        in_specs=(
            P("seq", None, "tensor"),
            P(None, None, "tensor"),
            P(None, "tensor"),
            P("seq", "tensor"),
            P(None, "tensor"),
            P("seq", "tensor"),
        ),
        out_specs=(
            P("seq", "tensor"),
            P("seq", None, "tensor"),
            P("seq", "tensor"),
            P(None, "tensor"),
            P(None, None, "tensor"),
        ),
        check_vma=False,
    )
```

profile of v0, /device:TPU:0, one launch (start us, length us, event | category | flops | bytes accessed | tf_op | source)
XLA Modules:
  0.0 607.2 jit_solution(8944364279748115227)
XLA Ops:
  8.7 4.9 collective-permute-start
  23.4 11.5 %all-gather.2.cloned.1.call-done = bf16[128,8192]{1,0:T(8,128)(2,1)} async-done(((bf16[128,2048]{1,0:T(8,128)(2,1)}), bf16[128,8192]{1,0:T(8,128)(2,1)}) %all-gather.2.cloned.1.call-update) | async-done | bytes 2097168 | tf_op jit(solution)/shard_map/all_gather | solution.py:157
  34.9 9.8 %slice_multiply_fusion.1 = (f32[128,1024]{1,0:T(8,128)}, f32[128,1024]{1,0:T(8,128)S(1)}, f32[128,1024]{1,0:T(8,128)}) fusion(f32[128,3072]{1,0:T(8,128)S(1)} %slice_bitcast_fusion, bf16[128,8192]{1,0:T(8,128)(2,1)} %all-gather.2.cloned.1.call-done, bf16[8192,1024]{1,0:T(8,128)(2,1)} %param.10), kind=kOutput, calls=%fused_computation.100 | convolution fusion | flops 2147745792 | bytes 22020096 | tf_op jit(solution)/shard_map/dot_general | solution.py:158
  48.4 4.6 all-to-all-start.4
  55.0 5.3 fusion.57
  61.7 5.9 all-to-all-done.4
  67.6 4.1 all-to-all-start
  77.5 20.0 %all-to-all-done = f32[2,8,16,1024]{3,2,0,1:T(8,128)S(1)} async-done(((f32[2,8,16,1024]{3,2,0,1:T(8,128)}), f32[2,8,16,1024]{3,2,0,1:T(8,128)S(1)}, u32[]{:S(2)}, u32[]{:S(2)}) %all-to-all-start) | async-done | bytes 1048608 | tf_op jit(solution)/shard_map/all_to_all | solution.py:50
  107.1 4.4 copy.127
  111.5 38.0 %all-to-all-done.5 = f32[2,1,16,16,1024]{4,3,1,0,2:T(8,128)S(1)} async-done(((f32[2,1,16,16,1024]{4,3,1,0,2:T(8,128)}), f32[2,1,16,16,1024]{4,3,1,0,2:T(8,128)S(1)}, u32[]{:S(2)}, u32[]{:S(2)}) %all-to-all-start.5) | async-done | bytes 2097184 | tf_op jit(solution)/shard_map/all_to_all | solution.py:72
  149.5 5.0 all-to-all-start.1
  163.1 83.5 %all-to-all-done.1 = f32[2,2,16,16,1024]{4,3,1,0,2:T(8,128)} async-done(((f32[2,2,16,16,1024]{4,3,1,0,2:T(8,128)}), f32[2,2,16,16,1024]{4,3,1,0,2:T(8,128)}, u32[]{:S(2)}, u32[]{:S(2)}) %all-to-all-start.1) | async-done | bytes 4194336 | tf_op jit(solution)/shard_map/all_to_all | solution.py:72
  279.1 7.3 %copy.150 = f32[2,2,2,128,1024]{4,2,1,0,3:T(2,128)} copy(f32[2,2,2,128,1024]{3,4,2,1,0:T(8,128)} %pad_maximum_fusion.1) | data formatting | bytes 8388608 | tf_op jit(solution)/shard_map/stack | solution.py:100
  286.4 4.6 all-to-all-start.6
  298.7 84.8 %all-to-all-done.6 = f32[2,2,2,128,1024]{4,2,1,0,3:T(2,128)} async-done(((f32[2,2,2,128,1024]{4,2,1,0,3:T(2,128)}), f32[2,2,2,128,1024]{4,2,1,0,3:T(2,128)}, u32[]{:S(2)}, u32[]{:S(2)}) %all-to-all-start.6) | async-done | bytes 4194336 | tf_op jit(solution)/shard_map/all_to_all | solution.py:106
  387.3 4.6 copy.151
  400.4 4.6 copy.153
  414.6 21.1 %all-to-all-done.2 = f32[2,1,2,128,1024]{4,2,1,0,3:T(2,128)S(1)} async-done(((f32[2,1,2,128,1024]{4,2,1,0,3:T(2,128)}), f32[2,1,2,128,1024]{4,2,1,0,3:T(2,128)S(1)}, u32[]{:S(2)}, u32[]{:S(2)}) %all-to-all-start.2) | async-done | bytes 2097184 | tf_op jit(solution)/shard_map/all_to_all | solution.py:106
  451.0 14.5 %all-to-all-done.7 = f32[2,8,16,1024]{3,2,0,1:T(8,128)S(1)} async-done(((f32[2,8,16,1024]{3,2,0,1:T(8,128)}), f32[2,8,16,1024]{3,2,0,1:T(8,128)S(1)}, u32[]{:S(2)}, u32[]{:S(2)}) %all-to-all-start.7) | async-done | bytes 1048608 | tf_op jit(solution)/shard_map/all_to_all | solution.py:114
  471.3 5.3 fusion.51
  484.2 6.2 %fusion.55 = f32[1,128,1024]{2,0,1:T(1,128)} fusion(f32[1,247,1024]{2,0,1:T(1,128)S(1)} %broadcast_in_dim.20, f32[120,1,1024]{2,0,1:T(8,128)S(1)} %bitcast.294), kind=kOutput, calls=%fused_computation.106 | convolution fusion | flops 188743680 | bytes 2027520 | tf_op jit(solution)/shard_map/conv_general_dilated | solution.py:26
  492.9 13.3 %fusion.276 = f32[128,8192]{1,0:T(8,128)} fusion(bf16[128,1024]{1,0:T(8,128)(2,1)S(1)} %get-tuple-element.49, bf16[8192,1024]{1,0:T(8,128)(2,1)} %param.10), kind=kOutput, calls=%fused_computation.310 | convolution fusion | flops 2147483648 | bytes 21233664 | tf_op jit(solution)/shard_map/dot_general | solution.py:151
  514.6 39.4 %psum.15 = bf16[7,3072]{1,0:T(8,128)(2,1)S(1)} all-reduce(bf16[7,3072]{1,0:T(8,128)(2,1)S(1)} %rev.15), channel_id=1, replica_groups=mesh['seq'=8,'tensor'=4] {'seq'}, use_global_device_ids=true, to_apply=%region_2.3 | all-reduce | flops 21504 | bytes 86016 | tf_op jit(solution)/shard_map/psum | solution.py:194
  562.9 35.2 %reduce-scatter.2.cloned.1.call-done = f32[128,2048]{1,0:T(8,128)} async-done(((f32[128,8192]{1,0:T(8,128)}), f32[128,2048]{1,0:T(8,128)}) %reduce-scatter.2.cloned.1.call-update) | async-done | bytes 1048592 | tf_op jit(solution)/shard_map/reduce_scatter | solution.py:154
  (164 shorter events, 154.1 us)
Async XLA Ops:
  7.2 8.0 %copy-start.15 = (f32[7,3,1024]{2,0,1:T(8,128)S(1)}, f32[7,3,1024]{2,0,1:T(8,128)}, u32[]{:S(2)}) copy-start(f32[7,3,1024]{2,0,1:T(8,128)} %param.7) | copy-start | bytes 258052
  7.2 27.7 %all-gather.2.cloned.1.call-start = ((), (), s32[]{:S(2)}) async-start(), calls=%async_computation.10 | async-start | bytes 2621440 | tf_op jit(solution)/shard_map/all_gather | solution.py:157
  8.7 7.1 %collective-permute-start = (bf16[6,3072]{1,0:T(8,128)(2,1)S(1)}, bf16[6,3072]{1,0:T(8,128)(2,1)S(1)}, u32[]{:S(2)}, u32[]{:S(2)}) collective-permute-start(bf16[6,3072]{1,0:T(8,128)(2,1)S(1)} %bitcast.300), channel_id=1, source_target_pairs={{0,4},{4,8},{8,12},{12,16},{16,20},{20,24},{24,28},{1,5},{5,9},{9,... | collective-permute-start | bytes 110600 | tf_op jit(solution)/shard_map/ppermute | solution.py:13
  23.4 21.3 %copy-start = (f32[128,3072]{1,0:T(8,128)}, f32[128,3072]{1,0:T(8,128)S(1)}, u32[]{:S(2)}) copy-start(f32[128,3072]{1,0:T(8,128)S(1)} %slice_bitcast_fusion) | copy-start | bytes 4718596
  23.4 24.7 %copy-start.13 = (f32[120,1024]{1,0:T(8,128)S(1)}, f32[120,1024]{1,0:T(8,128)}, u32[]{:S(2)}) copy-start(f32[120,1024]{1,0:T(8,128)} %param.8) | copy-start | bytes 1474564
  44.7 9.4 %collective-permute-start.1 = (bf16[119,1024]{1,0:T(8,128)(2,1)S(1)}, bf16[119,1024]{1,0:T(8,128)(2,1)S(1)}, u32[]{:S(2)}, u32[]{:S(2)}) collective-permute-start(bf16[119,1024]{1,0:T(8,128)(2,1)S(1)} %slice.165), channel_id=1, source_target_pairs={{0,4},{4,8},{8,12},{12,16},{16,20},{20,24},{24,28},{1,5},{5,9},{9,... | collective-permute-start | bytes 731144 | tf_op jit(solution)/shard_map/ppermute | solution.py:13
  48.4 19.2 %all-to-all-start.4 = ((f32[1,8,16,1024]{3,2,0,1:T(8,128)}), f32[1,8,16,1024]{3,2,0,1:T(8,128)S(1)}, u32[]{:S(2)}, u32[]{:S(2)}) async-start(f32[1,8,16,1024]{3,2,0,1:T(8,128)} %bitcast.49), calls=%async_computation.5 | async-start | bytes 1048576 | tf_op jit(solution)/shard_map/all_to_all | solution.py:50
  54.9 5.4 copy-start.10
  55.0 5.5 copy-start.12
  67.6 29.9 %all-to-all-start = ((f32[2,8,16,1024]{3,2,0,1:T(8,128)}), f32[2,8,16,1024]{3,2,0,1:T(8,128)S(1)}, u32[]{:S(2)}, u32[]{:S(2)}) async-start(f32[2,8,16,1024]{3,2,0,1:T(8,128)} %copy.124), calls=%async_computation | async-start | bytes 2097152 | tf_op jit(solution)/shard_map/all_to_all | solution.py:50
  97.5 52.1 %all-to-all-start.5 = ((f32[2,1,16,16,1024]{4,3,1,0,2:T(8,128)}), f32[2,1,16,16,1024]{4,3,1,0,2:T(8,128)S(1)}, u32[]{:S(2)}, u32[]{:S(2)}) async-start(f32[2,1,16,16,1024]{4,3,1,0,2:T(8,128)} %copy.142), calls=%async_computation.6 | async-start | bytes 4194304 | tf_op jit(solution)/shard_map/all_to_all | solution.py:72
  149.5 97.1 %all-to-all-start.1 = ((f32[2,2,16,16,1024]{4,3,1,0,2:T(8,128)}), f32[2,2,16,16,1024]{4,3,1,0,2:T(8,128)}, u32[]{:S(2)}, u32[]{:S(2)}) async-start(f32[2,2,16,16,1024]{4,3,1,0,2:T(8,128)} %copy.127), calls=%async_computation.1 | async-start | bytes 8388608 | tf_op jit(solution)/shard_map/all_to_all | solution.py:72
  261.2 3.7 copy-start.5
  286.4 97.1 %all-to-all-start.6 = ((f32[2,2,2,128,1024]{4,2,1,0,3:T(2,128)}), f32[2,2,2,128,1024]{4,2,1,0,3:T(2,128)}, u32[]{:S(2)}, u32[]{:S(2)}) async-start(f32[2,2,2,128,1024]{4,2,1,0,3:T(2,128)} %copy.150), calls=%async_computation.7 | async-start | bytes 8388608 | tf_op jit(solution)/shard_map/all_to_all | solution.py:106
  383.5 52.2 %all-to-all-start.2 = ((f32[2,1,2,128,1024]{4,2,1,0,3:T(2,128)}), f32[2,1,2,128,1024]{4,2,1,0,3:T(2,128)S(1)}, u32[]{:S(2)}, u32[]{:S(2)}) async-start(f32[2,1,2,128,1024]{4,2,1,0,3:T(2,128)} %copy.135), calls=%async_computation.2 | async-start | bytes 4194304 | tf_op jit(solution)/shard_map/all_to_all | solution.py:106
  435.7 29.8 %all-to-all-start.7 = ((f32[2,8,16,1024]{3,2,0,1:T(8,128)}), f32[2,8,16,1024]{3,2,0,1:T(8,128)S(1)}, u32[]{:S(2)}, u32[]{:S(2)}) async-start(f32[2,8,16,1024]{3,2,0,1:T(8,128)} %copy.154), calls=%async_computation.8 | async-start | bytes 2097152 | tf_op jit(solution)/shard_map/all_to_all | solution.py:114
  449.9 21.3 %copy-start.11 = (f32[1,247,1024]{2,0,1:T(1,128)S(1)}, f32[1,247,1024]{2,0,1:T(1,128)}, u32[]{:S(2)}) copy-start(f32[1,247,1024]{2,0,1:T(1,128)} %copy-done.10) | copy-start | bytes 3035140
  465.5 11.1 %copy-start.3 = (f32[2,8,16,1024]{3,2,0,1:T(8,128)}, f32[2,8,16,1024]{3,2,0,1:T(8,128)S(1)}, u32[]{:S(2)}) copy-start(f32[2,8,16,1024]{3,2,0,1:T(8,128)S(1)} %all-to-all-done.7) | copy-start | bytes 3145732
  465.5 24.9 %all-to-all-start.3 = ((f32[1,8,16,1024]{3,2,0,1:T(8,128)}), f32[1,8,16,1024]{3,2,0,1:T(8,128)S(1)}, u32[]{:S(2)}, u32[]{:S(2)}) async-start(f32[1,8,16,1024]{3,2,0,1:T(8,128)} %copy.139), calls=%async_computation.3 | async-start | bytes 1048576 | tf_op jit(solution)/shard_map/all_to_all | solution.py:114
  469.1 85.5 %all-reduce.2.cloned.1.call-start = ((), (), s32[]{:S(2)}) async-start(), calls=%async_computation.11 | async-start | bytes 491520 | tf_op jit(solution)/shard_map/psum | solution.py:193
  470.0 13.1 %collective-permute-start.2 = (bf16[119,1024]{1,0:T(8,128)(2,1)}, bf16[119,1024]{1,0:T(8,128)(2,1)S(1)}, u32[]{:S(2)}, u32[]{:S(2)}) collective-permute-start(bf16[119,1024]{1,0:T(8,128)(2,1)} %slice.164), channel_id=1, source_target_pairs={{4,0},{8,4},{12,8},{16,12},{20,16},{24,20},{28,24},{5,1},{9,5},{13... | collective-permute-start | bytes 731144 | tf_op jit(solution)/shard_map/ppermute | solution.py:13
  479.3 118.9 %reduce-scatter.2.cloned.1.call-start = ((), (), s32[]{:S(2)}) async-start(), calls=%async_computation.9 | async-start | bytes 5242880 | tf_op jit(solution)/shard_map/reduce_scatter | solution.py:154
  484.2 7.0 %copy-start.1 = (f32[128,3072]{1,0:T(8,128)S(1)}, f32[128,3072]{1,0:T(8,128)}, u32[]{:S(2)}) copy-start(f32[128,3072]{1,0:T(8,128)} %copy-done) | copy-start | bytes 4718596
  513.3 43.2 %collective-permute-start.3 = (bf16[6,3072]{1,0:T(8,128)(2,1)S(1)}, bf16[6,3072]{1,0:T(8,128)(2,1)S(1)}, u32[]{:S(2)}, u32[]{:S(2)}) collective-permute-start(bf16[6,3072]{1,0:T(8,128)(2,1)S(1)} %slice.166), channel_id=1, source_target_pairs={{4,0},{8,4},{12,8},{16,12},{20,16},{24,20},{28,24},{5,1},{9,5},{13... | collective-permute-start | bytes 110600 | tf_op jit(solution)/shard_map/ppermute | solution.py:13
  (10 other events, 14.8 us)
Sparse Core Ops, SparseCore 0:
  9.5 25.2 all-gather.1
  479.4 72.5 all-reduce.1
  554.6 43.5 reduce-scatter.1
where the time goes:
time: 616 us; the launch traced here: 607 us
  waiting for transfers between devices  320 us (52%)
  matrix products  98.7 us (16%)
  local copies, waits for them, and re-layouts  77.8 us (13%)
  starting transfers between devices  44.2 us (7%)
  blocking collectives  39.4 us (6%)
  between operations  15.1 us (2%)
  other arithmetic  11.9 us (2%)
    all_to_all x2, waiting for transfers between devices, to_spectrum(): lax.all_to_all(turned, 'seq', split_axis=2, concat_axis=3, tiled=True)  122 us
    all_to_all x2, waiting for transfers between devices, from_spectrum(): lax.all_to_all(turned, 'seq', split_axis=3, concat_axis=2, tiled=True)  106 us
    psum x1, blocking collectives, local(): lax.psum(short_part.astype(jnp.bfloat16), 'seq').astype(jnp.float32)  39.4 us
    reduce_scatter x1, waiting for transfers between devices, local(): lax.psum_scatter(partial_out, 'tensor', scatter_dimension=1, tiled=True)  35.2 us
    all_to_all x2, waiting for transfers between devices, to_spectrum(): lax.all_to_all(signals.reshape(signal_count, devices, stride, channels),...  25.9 us
    conv_general_dilated x6, matrix products, correlate(): lax.conv_general_dilated(signal[None], kernel[:, None, :], (1,), 'VALID',...  22.3 us
    all_to_all x2, waiting for transfers between devices, from_spectrum(): lax.all_to_all(blocks, 'seq', split_axis=1, concat_axis=1, tiled=True)  14.5 us
    dot_general x1, matrix products, local(): lax.dot_general(product, out_weight, (((1,), (1,)), ((), ())), preferred_...  13.3 us
  transfers between devices with their start and end apart: 15, of which 11 were waited for; matrix products, arithmetic and copies ran while one was open for 22% of the time, Pallas kernels for 0%

commit v1 on v0

--- a/solution.py
+++ b/solution.py
@@ -1,10 +1,22 @@
+import functools
 import math
 import jax
 import jax.numpy as jnp
 from jax import lax
 from jax.sharding import PartitionSpec as P
+from jax.lax import all_to_all, axis_size
 
 precise = lax.Precision.HIGHEST
+
+
+def resolve_lines_on(my_tile, axis_id, in_dim, on_dim):
+    return jnp.concatenate(
+        all_to_all(jnp.stack(jnp.split(my_tile, axis_size(axis_id), axis=in_dim)), axis_id, 0, 0),
+        axis=on_dim,
+    )
+
+
+part_kinds = functools.partial(resolve_lines_on, axis_id="seq", in_dim=2, on_dim=3)
 
 
 def from_behind(value, axis, steps):
@@ -69,7 +81,7 @@
             first_imag * cosine_values - first_real * sine_part,
         ]
     )
-    arrived = lax.all_to_all(turned, "seq", split_axis=2, concat_axis=3, tiled=True)
+    arrived = part_kinds(turned)
     spec_real = jnp.einsum("km,sjmc->sjkc", cos_table, arrived[0], precision=precise) + jnp.einsum(
         "km,sjmc->sjkc", sin_table, arrived[1], precision=precise
     )

time: 616 us -> 617 us (level)
  other arithmetic: 11.9 us -> 19.9 us
    unnamed x0 -> x7, other arithmetic: none -> 7.27 us
  transfers between devices with their start and end apart: 15 -> 15, of which waited for: 11 -> 11; matrix products, arithmetic and copies ran while one was open for 22% -> 23% of each run, Pallas kernels for 0% -> 0%
where the time goes in v1:
time: 617 us; the launch traced here: 608 us
  waiting for transfers between devices  316 us (51%)
  matrix products  96.1 us (16%)
  local copies, waits for them, and re-layouts  78.5 us (13%)
  starting transfers between devices  43.6 us (7%)
  blocking collectives  39.4 us (6%)
  other arithmetic  19.9 us (3%)
  between operations  15.2 us (2%)
    all_to_all x2, waiting for transfers between devices, resolve_lines_on(): all_to_all(jnp.stack(jnp.split(my_tile, axis_size(axis_id), axis=in_dim))...  116 us
    all_to_all x2, waiting for transfers between devices, from_spectrum(): lax.all_to_all(turned, 'seq', split_axis=3, concat_axis=2, tiled=True)  106 us
    psum x1, blocking collectives, local(): lax.psum(short_part.astype(jnp.bfloat16), 'seq').astype(jnp.float32)  39.4 us
    reduce_scatter x1, waiting for transfers between devices, local(): lax.psum_scatter(partial_out, 'tensor', scatter_dimension=1, tiled=True)  35.3 us
    all_to_all x2, waiting for transfers between devices, to_spectrum(): lax.all_to_all(signals.reshape(signal_count, devices, stride, channels),...  26.7 us
    conv_general_dilated x6, matrix products, correlate(): lax.conv_general_dilated(signal[None], kernel[:, None, :], (1,), 'VALID',...  22.3 us
    all_to_all x2, waiting for transfers between devices, from_spectrum(): lax.all_to_all(blocks, 'seq', split_axis=1, concat_axis=1, tiled=True)  14.5 us
    dot_general x1, matrix products, local(): lax.dot_general(product, out_weight, (((1,), (1,)), ((), ())), preferred_...  13.4 us
  transfers between devices with their start and end apart: 15, of which 11 were waited for; matrix products, arithmetic and copies ran while one was open for 23% of the time, Pallas kernels for 0%

profile of v1, /device:TPU:0, one launch (start us, length us, event | category | flops | bytes accessed | tf_op | source)
XLA Modules:
  0.0 608.2 jit_solution(10297950714115146025)
XLA Ops:
  8.7 4.9 collective-permute-start
  23.4 11.4 %all-gather.2.cloned.1.call-done = bf16[128,8192]{1,0:T(8,128)(2,1)} async-done(((bf16[128,2048]{1,0:T(8,128)(2,1)}), bf16[128,8192]{1,0:T(8,128)(2,1)}) %all-gather.2.cloned.1.call-update) | async-done | bytes 2097168 | tf_op jit(solution)/shard_map/all_gather | solution.py:169
  34.9 9.8 %slice_multiply_fusion.1 = (f32[128,1024]{1,0:T(8,128)}, f32[128,1024]{1,0:T(8,128)S(1)}, f32[128,1024]{1,0:T(8,128)}) fusion(f32[128,3072]{1,0:T(8,128)S(1)} %slice_bitcast_fusion, bf16[128,8192]{1,0:T(8,128)(2,1)} %all-gather.2.cloned.1.call-done, bf16[8192,1024]{1,0:T(8,128)(2,1)} %param.10), kind=kOutput, calls=%fused_computation.140 | convolution fusion | flops 2147745792 | bytes 22020096 | tf_op jit(solution)/shard_map/dot_general | solution.py:170
  48.5 4.6 all-to-all-start.4
  54.8 5.3 fusion.81
  61.5 6.2 %all-to-all-done.4 = f32[1,8,16,1024]{3,2,0,1:T(8,128)S(1)} async-done(((f32[1,8,16,1024]{3,2,0,1:T(8,128)}), f32[1,8,16,1024]{3,2,0,1:T(8,128)S(1)}, u32[]{:S(2)}, u32[]{:S(2)}) %all-to-all-start.4) | async-done | bytes 524320 | tf_op jit(solution)/shard_map/all_to_all | solution.py:62
  67.7 3.9 all-to-all-start
  77.1 20.5 %all-to-all-done = f32[2,8,16,1024]{3,2,0,1:T(8,128)S(1)} async-done(((f32[2,8,16,1024]{3,2,0,1:T(8,128)}), f32[2,8,16,1024]{3,2,0,1:T(8,128)S(1)}, u32[]{:S(2)}, u32[]{:S(2)}) %all-to-all-start) | async-done | bytes 1048608 | tf_op jit(solution)/shard_map/all_to_all | solution.py:62
  115.2 34.4 %all-to-all-done.5 = f32[8,2,1,2,16,1024]{5,3,4,1,2,0:T(2,128)S(1)} async-done(((f32[8,2,1,2,16,1024]{5,3,4,1,2,0:T(2,128)}), f32[8,2,1,2,16,1024]{5,3,4,1,2,0:T(2,128)S(1)}, u32[]{:S(2)}, u32[]{:S(2)}) %all-to-all-start.5) | async-done | bytes 2097184 | tf_op jit(solution)/shard_map/all_to_all | solution.py:14
  149.6 4.6 all-to-all-start.1
  164.7 82.1 %all-to-all-done.1 = f32[8,2,2,2,16,1024]{5,3,4,2,1,0:T(2,128)} async-done(((f32[8,2,2,2,16,1024]{5,3,4,2,1,0:T(2,128)}), f32[8,2,2,2,16,1024]{5,3,4,2,1,0:T(2,128)}, u32[]{:S(2)}, u32[]{:S(2)}) %all-to-all-start.1) | async-done | bytes 4194336 | tf_op jit(solution)/shard_map/all_to_all | solution.py:14
  280.0 7.3 %copy.119 = f32[2,2,2,128,1024]{4,2,1,0,3:T(2,128)} copy(f32[2,2,2,128,1024]{3,4,2,1,0:T(8,128)} %pad_maximum_fusion) | data formatting | bytes 8388608 | tf_op jit(solution)/shard_map/stack | solution.py:112
  287.3 4.5 all-to-all-start.6
  299.6 84.9 %all-to-all-done.6 = f32[2,2,2,128,1024]{4,2,1,0,3:T(2,128)} async-done(((f32[2,2,2,128,1024]{4,2,1,0,3:T(2,128)}), f32[2,2,2,128,1024]{4,2,1,0,3:T(2,128)}, u32[]{:S(2)}, u32[]{:S(2)}) %all-to-all-start.6) | async-done | bytes 4194336 | tf_op jit(solution)/shard_map/all_to_all | solution.py:118
  388.3 4.6 copy.120
  401.3 4.6 copy.122
  415.6 21.1 %all-to-all-done.2 = f32[2,1,2,128,1024]{4,2,1,0,3:T(2,128)S(1)} async-done(((f32[2,1,2,128,1024]{4,2,1,0,3:T(2,128)}), f32[2,1,2,128,1024]{4,2,1,0,3:T(2,128)S(1)}, u32[]{:S(2)}, u32[]{:S(2)}) %all-to-all-start.2) | async-done | bytes 2097184 | tf_op jit(solution)/shard_map/all_to_all | solution.py:118
  436.7 3.9 all-to-all-start.7
  452.0 14.5 %all-to-all-done.7 = f32[2,8,16,1024]{3,2,0,1:T(8,128)S(1)} async-done(((f32[2,8,16,1024]{3,2,0,1:T(8,128)}), f32[2,8,16,1024]{3,2,0,1:T(8,128)S(1)}, u32[]{:S(2)}, u32[]{:S(2)}) %all-to-all-start.7) | async-done | bytes 1048608 | tf_op jit(solution)/shard_map/all_to_all | solution.py:126
  472.2 5.3 fusion.75
  485.1 6.2 %fusion.79 = f32[1,128,1024]{2,0,1:T(1,128)} fusion(f32[1,247,1024]{2,0,1:T(1,128)S(1)} %broadcast_in_dim.20, f32[120,1,1024]{2,0,1:T(8,128)S(1)} %bitcast.359), kind=kOutput, calls=%fused_computation.146 | convolution fusion | flops 188743680 | bytes 2027520 | tf_op jit(solution)/shard_map/conv_general_dilated | solution.py:38
  493.8 13.4 %fusion.310 = f32[128,8192]{1,0:T(8,128)} fusion(bf16[128,1024]{1,0:T(8,128)(2,1)S(1)} %get-tuple-element.44, bf16[8192,1024]{1,0:T(8,128)(2,1)} %param.10), kind=kOutput, calls=%fused_computation.367 | convolution fusion | flops 2147483648 | bytes 21233664 | tf_op jit(solution)/shard_map/dot_general | solution.py:163
  515.6 39.4 %psum.15 = bf16[7,3072]{1,0:T(8,128)(2,1)S(1)} all-reduce(bf16[7,3072]{1,0:T(8,128)(2,1)S(1)} %rev.15), channel_id=1, replica_groups=mesh['seq'=8,'tensor'=4] {'seq'}, use_global_device_ids=true, to_apply=%region_2.3 | all-reduce | flops 21504 | bytes 86016 | tf_op jit(solution)/shard_map/psum | solution.py:206
  563.8 35.3 %reduce-scatter.2.cloned.1.call-done = f32[128,2048]{1,0:T(8,128)} async-done(((f32[128,8192]{1,0:T(8,128)}), f32[128,2048]{1,0:T(8,128)}) %reduce-scatter.2.cloned.1.call-update) | async-done | bytes 1048592 | tf_op jit(solution)/shard_map/reduce_scatter | solution.py:166
  (179 shorter events, 160.4 us)
Async XLA Ops:
  7.2 8.0 %copy-start.17 = (f32[7,3,1024]{2,0,1:T(8,128)S(1)}, f32[7,3,1024]{2,0,1:T(8,128)}, u32[]{:S(2)}) copy-start(f32[7,3,1024]{2,0,1:T(8,128)} %param.7) | copy-start | bytes 258052
  7.2 27.7 %all-gather.2.cloned.1.call-start = ((), (), s32[]{:S(2)}) async-start(), calls=%async_computation.10 | async-start | bytes 2621440 | tf_op jit(solution)/shard_map/all_gather | solution.py:169
  8.7 7.1 %collective-permute-start = (bf16[6,3072]{1,0:T(8,128)(2,1)S(1)}, bf16[6,3072]{1,0:T(8,128)(2,1)S(1)}, u32[]{:S(2)}, u32[]{:S(2)}) collective-permute-start(bf16[6,3072]{1,0:T(8,128)(2,1)S(1)} %bitcast.365), channel_id=1, source_target_pairs={{0,4},{4,8},{8,12},{12,16},{16,20},{20,24},{24,28},{1,5},{5,9},{9,... | collective-permute-start | bytes 110600 | tf_op jit(solution)/shard_map/ppermute | solution.py:25
  23.4 21.2 %copy-start = (f32[128,3072]{1,0:T(8,128)}, f32[128,3072]{1,0:T(8,128)S(1)}, u32[]{:S(2)}) copy-start(f32[128,3072]{1,0:T(8,128)S(1)} %slice_bitcast_fusion) | copy-start | bytes 4718596
  23.4 24.7 %copy-start.15 = (f32[120,1024]{1,0:T(8,128)S(1)}, f32[120,1024]{1,0:T(8,128)}, u32[]{:S(2)}) copy-start(f32[120,1024]{1,0:T(8,128)} %param.8) | copy-start | bytes 1474564
  44.7 9.3 %collective-permute-start.1 = (bf16[119,1024]{1,0:T(8,128)(2,1)S(1)}, bf16[119,1024]{1,0:T(8,128)(2,1)S(1)}, u32[]{:S(2)}, u32[]{:S(2)}) collective-permute-start(bf16[119,1024]{1,0:T(8,128)(2,1)S(1)} %slice.165), channel_id=1, source_target_pairs={{0,4},{4,8},{8,12},{12,16},{16,20},{20,24},{24,28},{1,5},{5,9},{9,... | collective-permute-start | bytes 731144 | tf_op jit(solution)/shard_map/ppermute | solution.py:25
  48.5 19.2 %all-to-all-start.4 = ((f32[1,8,16,1024]{3,2,0,1:T(8,128)}), f32[1,8,16,1024]{3,2,0,1:T(8,128)S(1)}, u32[]{:S(2)}, u32[]{:S(2)}) async-start(f32[1,8,16,1024]{3,2,0,1:T(8,128)} %bitcast.55), calls=%async_computation.5 | async-start | bytes 1048576 | tf_op jit(solution)/shard_map/all_to_all | solution.py:62
  54.8 5.4 copy-start.12
  54.8 5.5 copy-start.14
  67.7 29.9 %all-to-all-start = ((f32[2,8,16,1024]{3,2,0,1:T(8,128)}), f32[2,8,16,1024]{3,2,0,1:T(8,128)S(1)}, u32[]{:S(2)}, u32[]{:S(2)}) async-start(f32[2,8,16,1024]{3,2,0,1:T(8,128)} %copy.92), calls=%async_computation | async-start | bytes 2097152 | tf_op jit(solution)/shard_map/all_to_all | solution.py:62
  97.6 52.1 %all-to-all-start.5 = ((f32[8,2,1,2,16,1024]{5,3,4,1,2,0:T(2,128)}), f32[8,2,1,2,16,1024]{5,3,4,1,2,0:T(2,128)S(1)}, u32[]{:S(2)}, u32[]{:S(2)}) async-start(f32[8,2,1,2,16,1024]{5,3,4,1,2,0:T(2,128)} %copy-done.10), calls=%async_computation.6 | async-start | bytes 4194304 | tf_op jit(solution)/shard_map/all_to_all | solution.py:14
  149.6 97.1 %all-to-all-start.1 = ((f32[8,2,2,2,16,1024]{5,3,4,2,1,0:T(2,128)}), f32[8,2,2,2,16,1024]{5,3,4,2,1,0:T(2,128)}, u32[]{:S(2)}, u32[]{:S(2)}) async-start(f32[8,2,2,2,16,1024]{5,3,4,2,1,0:T(2,128)} %fusion.71), calls=%async_computation.1 | async-start | bytes 8388608 | tf_op jit(solution)/shard_map/all_to_all | solution.py:14
  262.8 3.7 copy-start.6
  287.3 97.1 %all-to-all-start.6 = ((f32[2,2,2,128,1024]{4,2,1,0,3:T(2,128)}), f32[2,2,2,128,1024]{4,2,1,0,3:T(2,128)}, u32[]{:S(2)}, u32[]{:S(2)}) async-start(f32[2,2,2,128,1024]{4,2,1,0,3:T(2,128)} %copy.119), calls=%async_computation.7 | async-start | bytes 8388608 | tf_op jit(solution)/shard_map/all_to_all | solution.py:118
  384.5 52.2 %all-to-all-start.2 = ((f32[2,1,2,128,1024]{4,2,1,0,3:T(2,128)}), f32[2,1,2,128,1024]{4,2,1,0,3:T(2,128)S(1)}, u32[]{:S(2)}, u32[]{:S(2)}) async-start(f32[2,1,2,128,1024]{4,2,1,0,3:T(2,128)} %copy.101), calls=%async_computation.2 | async-start | bytes 4194304 | tf_op jit(solution)/shard_map/all_to_all | solution.py:118
  436.7 29.8 %all-to-all-start.7 = ((f32[2,8,16,1024]{3,2,0,1:T(8,128)}), f32[2,8,16,1024]{3,2,0,1:T(8,128)S(1)}, u32[]{:S(2)}, u32[]{:S(2)}) async-start(f32[2,8,16,1024]{3,2,0,1:T(8,128)} %copy.123), calls=%async_computation.8 | async-start | bytes 2097152 | tf_op jit(solution)/shard_map/all_to_all | solution.py:126
  450.8 21.4 %copy-start.13 = (f32[1,247,1024]{2,0,1:T(1,128)S(1)}, f32[1,247,1024]{2,0,1:T(1,128)}, u32[]{:S(2)}) copy-start(f32[1,247,1024]{2,0,1:T(1,128)} %copy-done.12) | copy-start | bytes 3035140
  466.4 11.1 %copy-start.3 = (f32[2,8,16,1024]{3,2,0,1:T(8,128)}, f32[2,8,16,1024]{3,2,0,1:T(8,128)S(1)}, u32[]{:S(2)}) copy-start(f32[2,8,16,1024]{3,2,0,1:T(8,128)S(1)} %all-to-all-done.7) | copy-start | bytes 3145732
  466.4 24.9 %all-to-all-start.3 = ((f32[1,8,16,1024]{3,2,0,1:T(8,128)}), f32[1,8,16,1024]{3,2,0,1:T(8,128)S(1)}, u32[]{:S(2)}, u32[]{:S(2)}) async-start(f32[1,8,16,1024]{3,2,0,1:T(8,128)} %copy.105), calls=%async_computation.3 | async-start | bytes 1048576 | tf_op jit(solution)/shard_map/all_to_all | solution.py:126
  470.1 85.5 %all-reduce.2.cloned.1.call-start = ((), (), s32[]{:S(2)}) async-start(), calls=%async_computation.11 | async-start | bytes 491520 | tf_op jit(solution)/shard_map/psum | solution.py:205
  470.9 13.1 %collective-permute-start.2 = (bf16[119,1024]{1,0:T(8,128)(2,1)}, bf16[119,1024]{1,0:T(8,128)(2,1)S(1)}, u32[]{:S(2)}, u32[]{:S(2)}) collective-permute-start(bf16[119,1024]{1,0:T(8,128)(2,1)} %slice.164), channel_id=1, source_target_pairs={{4,0},{8,4},{12,8},{16,12},{20,16},{24,20},{28,24},{5,1},{9,5},{13... | collective-permute-start | bytes 731144 | tf_op jit(solution)/shard_map/ppermute | solution.py:25
  480.3 118.9 %reduce-scatter.2.cloned.1.call-start = ((), (), s32[]{:S(2)}) async-start(), calls=%async_computation.9 | async-start | bytes 5242880 | tf_op jit(solution)/shard_map/reduce_scatter | solution.py:166
  485.1 7.0 %copy-start.1 = (f32[128,3072]{1,0:T(8,128)S(1)}, f32[128,3072]{1,0:T(8,128)}, u32[]{:S(2)}) copy-start(f32[128,3072]{1,0:T(8,128)} %copy-done) | copy-start | bytes 4718596
  514.3 43.1 %collective-permute-start.3 = (bf16[6,3072]{1,0:T(8,128)(2,1)S(1)}, bf16[6,3072]{1,0:T(8,128)(2,1)S(1)}, u32[]{:S(2)}, u32[]{:S(2)}) collective-permute-start(bf16[6,3072]{1,0:T(8,128)(2,1)S(1)} %slice.166), channel_id=1, source_target_pairs={{4,0},{8,4},{12,8},{16,12},{20,16},{24,20},{28,24},{5,1},{9,5},{13... | collective-permute-start | bytes 110600 | tf_op jit(solution)/shard_map/ppermute | solution.py:25
  (12 other events, 17.7 us)
Sparse Core Ops, SparseCore 0:
  9.5 25.2 all-gather.1
  480.4 72.5 all-reduce.1
  555.6 43.5 reduce-scatter.1
